TPU v7x, 32 devices: a whole 2x2x4 slice. The times are simulated.
32 devices in a mesh: lon: 8 (over y, x, core), lat: 4 (over z).
Axes of the slice: x: 2, y: 2, z: 4, core: 2. Of those that a mesh axis runs over, the one named last changes fastest.
Arguments:
- fields: float32 [5, 1, 128, 11520], P(None, None, 'lat', 'lon'), may hold values from -6 to 6
- frac_x: float32 [2, 1, 128], replicated, may hold values from 0.05 to 0.95
- frac_y: float32 [2, 1, 128], replicated, may hold values from 0.05 to 0.9
- shift_cells: int32 [2, 1, 128], replicated, may hold values from -5760 to 5759, as said below
- polar_mask: int32 [128], replicated, may hold values from 0 to 1, as said below
Outputs:
- fields_out: float32 [5, 1, 128, 11520], P(None, None, 'lat', 'lon')
Inputs may be any that keep to these rules, and one draw needn't show every extreme that they name: `shift_cells`: outside the first and last 32 rows every count lies in -2 .. 1, and both -2 and 1 occur there. `polar_mask`: nonzero only in the first and last 32 rows; the first and the last row are 1.
All inputs are finite; a program needn't handle non-finite values.
Results may differ from a plain program's by a relative error of at most 0.00016.
Values sent between devices are 32-bit elements; how exact they have to be, the bound alone decides.
A program may use at most 64 MiB of HBM per device.

v0:
```python
import math
import jax
import jax.numpy as jnp
from jax import lax
from jax.sharding import PartitionSpec as P

FA = 90
FB = 128
SUBS = 2
REACH = 4


def passed_along(x, axis, by):
    devices = lax.axis_size(axis)
    return lax.ppermute(x, axis, [(i, (i + by) % devices) for i in range(devices)])


def passed_along_2(block, axis, distance):
    devices = range(lax.axis_size(axis))
    route = [(i - distance, i) for i in devices if i - distance in devices]
    return lax.ppermute(block, axis, route)


def roll_digits(values, amount, span, axis):
    bit_total = max((span - 1).bit_length(), 1)
    for bit in range(bit_total):
        moved = jnp.roll(values, 1 << bit, axis=axis)
        taken = amount >> bit & 1 == 1
        values = jnp.where(taken, moved, values)
    return values


def cycle_move(state, counts, lon_cells):
    device_jump = jnp.floor_divide(counts, lon_cells)
    remainder = counts - device_jump * lon_cells
    select = device_jump + REACH
    bit_count = (2 * REACH).bit_length() - 1
    offsets = [-REACH] + [1 << bit for bit in range(bit_count)]
    current = state
    for turn, offset in enumerate(offsets):
        moved = passed_along(current, "lon", offset)
        if turn == 0:
            current = moved
        else:
            taken = select >> turn - 1 & 1 == 1
            current = jnp.where(taken[None, :, :, None], moved, current)
    western = passed_along(current, "lon", 1)
    joined = jnp.concatenate([western, current], axis=3)
    rolled = roll_digits(joined, remainder[None, :, :, None], lon_cells, 3)
    return rolled[:, :, :, lon_cells:]


def zonal_fraction(whole, courant):
    previous = jnp.roll(whole, 1, axis=1)
    edge = whole + 0.5 * (1.0 - courant) * (whole - previous)
    return whole - courant * (edge - jnp.roll(edge, 1, axis=1))


def polar_smooth(whole, lat_rows, marks, lat_cells, lat_total):
    row_count, lon_total = whole.shape
    highest = lax.Precision.HIGHEST
    first_ids = jnp.arange(FA, dtype=jnp.int32)
    second_ids = jnp.arange(FB, dtype=jnp.int32)
    angle_first = (
        2.0 * math.pi * (first_ids[:, None] * first_ids[None, :] % FA).astype(jnp.float32) / FA
    )
    cos_first, sin_first = (jnp.cos(angle_first), jnp.sin(angle_first))
    angle_second = (
        2.0 * math.pi * (second_ids[:, None] * second_ids[None, :] % FB).astype(jnp.float32) / FB
    )
    cos_second, sin_second = (jnp.cos(angle_second), jnp.sin(angle_second))
    angle_twist = (
        2.0
        * math.pi
        * (first_ids[:, None] * second_ids[None, :] % lon_total).astype(jnp.float32)
        / lon_total
    )
    cos_twist, sin_twist = (jnp.cos(angle_twist), jnp.sin(angle_twist))
    waves = (first_ids[:, None] + FA * second_ids[None, :]).astype(jnp.float32)
    sine = jnp.sin(math.pi * waves / lon_total)
    phi = math.pi * (lat_rows.astype(jnp.float32) + 0.5) / lat_total - math.pi / 2
    edge_cos = math.sin(math.pi * (lat_cells - 0.5) / lat_total)
    b_val = jnp.cos(phi) / edge_cos
    gain = 1.0 / (1.0 + sine[None, :, :] ** 2 / b_val[:, None, None] ** 2)
    grid = whole.reshape(row_count, FA, FB)
    real_one = jnp.einsum("kn,rnm->rkm", cos_first, grid, precision=highest)
    imag_one = -jnp.einsum("kn,rnm->rkm", sin_first, grid, precision=highest)
    real_two = real_one * cos_twist + imag_one * sin_twist
    imag_two = imag_one * cos_twist - real_one * sin_twist
    real_spec = jnp.einsum("rkm,mq->rkq", real_two, cos_second, precision=highest) + jnp.einsum(
        "rkm,mq->rkq", imag_two, sin_second, precision=highest
    )
    imag_spec = jnp.einsum("rkm,mq->rkq", imag_two, cos_second, precision=highest) - jnp.einsum(
        "rkm,mq->rkq", real_two, sin_second, precision=highest
    )
    real_spec = real_spec * gain
    imag_spec = imag_spec * gain
    real_back = jnp.einsum("rkq,mq->rkm", real_spec, cos_second, precision=highest) - jnp.einsum(
        "rkq,mq->rkm", imag_spec, sin_second, precision=highest
    )
    imag_back = jnp.einsum("rkq,mq->rkm", imag_spec, cos_second, precision=highest) + jnp.einsum(
        "rkq,mq->rkm", real_spec, sin_second, precision=highest
    )
    real_turn = real_back * cos_twist - imag_back * sin_twist
    imag_turn = imag_back * cos_twist + real_back * sin_twist
    result = jnp.einsum("kn,rkm->rnm", cos_first, real_turn, precision=highest) - jnp.einsum(
        "kn,rkm->rnm", sin_first, imag_turn, precision=highest
    )
    result = result.reshape(row_count, lon_total) / lon_total
    return jnp.where((marks == 1)[:, None], result, whole)


def meridional(state, merid_step, first_row):
    n_fields, n_levels, lat_cells, lon_cells = state.shape
    southern = passed_along_2(state[:, :, lat_cells - 2 :, :], "lat", 1)
    extended = jnp.concatenate([southern, state], axis=2)
    padded_faces = jnp.concatenate([merid_step, jnp.zeros((n_levels, 1), jnp.float32)], axis=1)
    faces = lax.dynamic_slice_in_dim(padded_faces, first_row, lat_cells + 1, 1)
    face_ids = first_row + jnp.arange(lat_cells + 1, dtype=jnp.int32)
    faces = jnp.where((face_ids == 0)[None, :], jnp.zeros_like(faces), faces)
    courant = faces[None, :, :, None]
    upper = extended[:, :, 1 : lat_cells + 2, :]
    lower = extended[:, :, 0 : lat_cells + 1, :]
    flux = courant * (upper + 0.5 * (1.0 - courant) * (upper - lower))
    return state + flux[:, :, :lat_cells, :] - flux[:, :, 1:, :]


def body(fields, frac_x, frac_y, shift_cells, polar_mask):
    n_fields, n_levels, lat_cells, lon_cells = fields.shape
    lon_devs = lax.axis_size("lon")
    lat_total = lat_cells * lax.axis_size("lat")
    lon_index = lax.axis_index("lon")
    first_row = lax.axis_index("lat") * lat_cells
    row_total = n_fields * n_levels * lat_cells
    per_device = row_total // lon_devs
    row_start = lon_index * per_device
    local_rows = first_row + jnp.arange(lat_cells, dtype=jnp.int32)
    marks_local = lax.dynamic_slice_in_dim(polar_mask, first_row, lat_cells, 0)

    def my_rows(table):
        spread = jnp.broadcast_to(table[None], (n_fields, n_levels, lat_cells)).reshape(row_total)
        return lax.dynamic_slice_in_dim(spread, row_start, per_device, 0)

    row_lats = my_rows(local_rows[None])
    row_marks = my_rows(marks_local[None])
    state = fields
    for substep in range(SUBS):
        counts = lax.dynamic_slice_in_dim(shift_cells[substep], first_row, lat_cells, 1)
        fractions = lax.dynamic_slice_in_dim(frac_x[substep], first_row, lat_cells, 1)
        placed = cycle_move(state, counts, lon_cells)
        flat = placed.reshape(row_total, lon_cells)
        whole = lax.all_to_all(flat, "lon", split_axis=0, concat_axis=1, tiled=True)
        whole = zonal_fraction(whole, my_rows(fractions)[:, None])
        whole = polar_smooth(whole, row_lats, row_marks, lat_cells, lat_total)
        blocks = lax.all_to_all(whole, "lon", split_axis=1, concat_axis=0, tiled=True)
        state = blocks.reshape(n_fields, n_levels, lat_cells, lon_cells)
        state = meridional(state, frac_y[substep], first_row)
    return state


def solution(mesh):
    return jax.shard_map(
        body,
        mesh=mesh,
        in_specs=(P(None, None, "lat", "lon"), P(), P(), P(), P()),
        out_specs=P(None, None, "lat", "lon"),
        check_vma=False,
    )
```

profile of v0, /device:TPU:0, one launch (start us, length us, event | category | flops | bytes accessed | tf_op | source)
XLA Modules:
  0.0 374.6 jit_solution(14722888508883360047)
XLA Ops:
  0.0 3.0 collective-permute-start
  3.0 22.0 %collective-permute-done = f32[5,1,32,1440]{3,2,1,0:T(8,128)S(1)} collective-permute-done((f32[5,1,32,1440]{3,2,1,0:T(8,128)}, f32[5,1,32,1440]{3,2,1,0:T(8,128)S(1)}, u32[]{:S(2)}, u32[]{:S(2)}) %collective-permute-start) | collective-permute-done | bytes 921632 | tf_op jit(solution)/shard_map/ppermute | solution.py:15
  26.3 13.1 %collective-permute-done.1 = f32[5,1,32,1440]{3,2,1,0:T(8,128)S(1)} collective-permute-done((f32[5,1,32,1440]{3,2,1,0:T(8,128)S(1)}, f32[5,1,32,1440]{3,2,1,0:T(8,128)S(1)}, u32[]{:S(2)}, u32[]{:S(2)}) %collective-permute-start.1) | collective-permute-done | bytes 921632 | tf_op jit(solution)/shard_map/ppermute | solution.py:15
  40.4 22.2 %collective-permute-done.2 = f32[5,1,32,1440]{3,2,1,0:T(8,128)S(1)} collective-permute-done((f32[5,1,32,1440]{3,2,1,0:T(8,128)S(1)}, f32[5,1,32,1440]{3,2,1,0:T(8,128)S(1)}, u32[]{:S(2)}, u32[]{:S(2)}) %collective-permute-start.2) | collective-permute-done | bytes 921632 | tf_op jit(solution)/shard_map/ppermute | solution.py:15
  62.8 1.6 collective-permute-start.3
  64.4 19.7 %collective-permute-done.3 = f32[5,1,32,1440]{3,2,1,0:T(8,128)S(1)} collective-permute-done((f32[5,1,32,1440]{3,2,1,0:T(8,128)S(1)}, f32[5,1,32,1440]{3,2,1,0:T(8,128)S(1)}, u32[]{:S(2)}, u32[]{:S(2)}) %collective-permute-start.3) | collective-permute-done | bytes 921632 | tf_op jit(solution)/shard_map/ppermute | solution.py:15
  85.2 13.6 %collective-permute-done.4 = f32[5,1,32,1440]{3,2,1,0:T(8,128)S(1)} collective-permute-done((f32[5,1,32,1440]{3,2,1,0:T(8,128)S(1)}, f32[5,1,32,1440]{3,2,1,0:T(8,128)S(1)}, u32[]{:S(2)}, u32[]{:S(2)}) %collective-permute-start.4) | collective-permute-done | bytes 921632 | tf_op jit(solution)/shard_map/ppermute | solution.py:15
  107.5 3.8 %all-to-all-start = ((f32[8,20,1440]{2,1,0:T(8,128)}), f32[8,20,1440]{2,1,0:T(8,128)S(1)}, u32[]{:S(2)}, u32[]{:S(2)}) async-start(f32[8,20,1440]{2,1,0:T(8,128)} %all_to_all.52), calls=%async_computation | async-start | bytes 2359296 | tf_op jit(solution)/shard_map/all_to_all | solution.py:152
  112.8 15.0 %all-to-all-done = f32[8,20,1440]{2,1,0:T(8,128)S(1)} async-done(((f32[8,20,1440]{2,1,0:T(8,128)}), f32[8,20,1440]{2,1,0:T(8,128)S(1)}, u32[]{:S(2)}, u32[]{:S(2)}) %all-to-all-start) | async-done | bytes 921632 | tf_op jit(solution)/shard_map/all_to_all | solution.py:152
  128.4 1.4 all_to_all.55
  131.2 1.6 concatenate.853
  134.1 1.6 concatenate.852
  136.8 2.1 multiply_subtract_fusion.3
  138.9 1.2 fusion.13
  140.1 1.2 convolution_bitcast_fusion.1
  143.7 1.2 fusion.11
  144.9 1.6 fusion.75
  146.5 1.2 fusion.12
  151.2 1.3 fusion.42
  152.5 2.3 fusion.10
  154.8 2.9 div.293
  157.7 4.0 %copy_select_fusion.1 = f32[20,8,1440]{2,0,1:T(8,128)} fusion(f32[20,8,1440]{2,1,0:T(8,128)} %div.293, f32[20,8,1440]{2,1,0:T(8,128)S(1)} %copy-done.2, f32[20,8,1440]{2,1,0:T(8,128)S(1)} %copy-done.3, f32[20]{0:T(128)S(1)} %get-tuple-element.18, f32[20]{0:T(128)S(1)} %get-tuple-element.19, pred[20]{0:T(512)(128)(4,1)S(1)} %dynamic-slice_compare_fusion, ...), kind=kLoop, calls=%fused_computation.69 | loop fusion | flops 1612800 | bytes 4608180 | tf_op jit(solution)/shard_map/jit(_where)/select_n | solution.py:110
  161.7 3.7 all-to-all-start.1
  166.0 16.2 %all-to-all-done.1 = f32[20,8,1440]{2,0,1:T(8,128)S(1)} async-done(((f32[20,8,1440]{2,0,1:T(8,128)}), f32[20,8,1440]{2,0,1:T(8,128)S(1)}, u32[]{:S(2)}, u32[]{:S(2)}) %all-to-all-start.1) | async-done | bytes 921632 | tf_op jit(solution)/shard_map/all_to_all | solution.py:155
  182.3 3.3 collective-permute-start.5
  185.6 1.8 collective-permute-done.5
  188.6 19.2 %collective-permute-done.6 = f32[5,1,32,1440]{3,2,0,1:T(8,128)S(1)} collective-permute-done((f32[5,1,32,1440]{3,2,0,1:T(8,128)S(1)}, f32[5,1,32,1440]{3,2,0,1:T(8,128)S(1)}, u32[]{:S(2)}, u32[]{:S(2)}) %collective-permute-start.6) | collective-permute-done | bytes 921632 | tf_op jit(solution)/shard_map/ppermute | solution.py:15
  207.9 14.4 %collective-permute-done.7 = f32[5,1,32,1440]{3,2,0,1:T(8,128)S(1)} collective-permute-done((f32[5,1,32,1440]{3,2,0,1:T(8,128)S(1)}, f32[5,1,32,1440]{3,2,0,1:T(8,128)S(1)}, u32[]{:S(2)}, u32[]{:S(2)}) %collective-permute-start.7) | collective-permute-done | bytes 921632 | tf_op jit(solution)/shard_map/ppermute | solution.py:15
  222.5 2.9 collective-permute-start.8
  225.4 22.2 %collective-permute-done.8 = f32[5,1,32,1440]{3,2,0,1:T(8,128)S(1)} collective-permute-done((f32[5,1,32,1440]{3,2,0,1:T(8,128)S(1)}, f32[5,1,32,1440]{3,2,0,1:T(8,128)S(1)}, u32[]{:S(2)}, u32[]{:S(2)}) %collective-permute-start.8) | collective-permute-done | bytes 921632 | tf_op jit(solution)/shard_map/ppermute | solution.py:15
  248.2 22.8 %collective-permute-done.9 = f32[5,1,32,1440]{3,2,0,1:T(8,128)S(1)} collective-permute-done((f32[5,1,32,1440]{3,2,0,1:T(8,128)S(1)}, f32[5,1,32,1440]{3,2,0,1:T(8,128)S(1)}, u32[]{:S(2)}, u32[]{:S(2)}) %collective-permute-start.9) | collective-permute-done | bytes 921632 | tf_op jit(solution)/shard_map/ppermute | solution.py:15
  271.4 14.3 %collective-permute-done.10 = f32[5,1,32,1440]{3,2,0,1:T(8,128)S(1)} collective-permute-done((f32[5,1,32,1440]{3,2,0,1:T(8,128)S(1)}, f32[5,1,32,1440]{3,2,0,1:T(8,128)S(1)}, u32[]{:S(2)}, u32[]{:S(2)}) %collective-permute-start.10) | collective-permute-done | bytes 921632 | tf_op jit(solution)/shard_map/ppermute | solution.py:15
  294.5 3.8 %all-to-all-start.2 = ((f32[8,20,1440]{2,1,0:T(8,128)}), f32[8,20,1440]{2,1,0:T(8,128)S(1)}, u32[]{:S(2)}, u32[]{:S(2)}) async-start(f32[8,20,1440]{2,1,0:T(8,128)} %all_to_all.59), calls=%async_computation.2 | async-start | bytes 2359296 | tf_op jit(solution)/shard_map/all_to_all | solution.py:152
  298.4 16.3 %all-to-all-done.2 = f32[8,20,1440]{2,1,0:T(8,128)S(1)} async-done(((f32[8,20,1440]{2,1,0:T(8,128)}), f32[8,20,1440]{2,1,0:T(8,128)S(1)}, u32[]{:S(2)}, u32[]{:S(2)}) %all-to-all-start.2) | async-done | bytes 921632 | tf_op jit(solution)/shard_map/all_to_all | solution.py:152
  315.3 1.4 all_to_all.62
  318.2 1.6 concatenate.873
  321.0 1.6 concatenate.872
  323.8 2.1 multiply_subtract_fusion.1
  325.9 1.2 fusion.8
  330.6 1.2 fusion.6
  333.0 1.4 fusion.7
  338.0 1.3 fusion.35
  339.3 2.3 fusion.5
  341.6 2.9 div.296
  344.5 2.9 copy_select_fusion
  347.5 19.2 %all_to_all.70 = f32[20,8,1440]{2,0,1:T(8,128)S(1)} all-to-all(f32[20,8,1440]{2,0,1:T(8,128)S(1)} %copy_select_fusion), channel_id=1, replica_groups=mesh['lon'=8,'lat'=4] {'lon'}, dimensions={1} | all-to-all | bytes 1843200 | tf_op jit(solution)/shard_map/all_to_all | solution.py:155
  366.8 4.0 %collective-permute-start.11 = (f32[5,1,2,1440]{3,2,0,1:T(2,128)S(1)}, f32[5,1,2,1440]{3,2,0,1:T(2,128)S(1)}, u32[]{:S(2)}, u32[]{:S(2)}) collective-permute-start(f32[5,1,2,1440]{3,2,0,1:T(2,128)S(1)} %slice.367), channel_id=1, source_target_pairs={{0,1},{1,2},{2,3},{4,5},{5,6},{6,7},{8,9},{9,10},{10,11},{12,13},{... | collective-permute-start | bytes 172808 | tf_op jit(solution)/shard_map/ppermute | solution.py:21
  370.8 1.8 collective-permute-done.11
  (164 shorter events, 50.0 us)
Async XLA Ops:
  0.0 24.9 %collective-permute-start = (f32[5,1,32,1440]{3,2,1,0:T(8,128)}, f32[5,1,32,1440]{3,2,1,0:T(8,128)S(1)}, u32[]{:S(2)}, u32[]{:S(2)}) collective-permute-start(f32[5,1,32,1440]{3,2,1,0:T(8,128)} %param.5), channel_id=1, source_target_pairs={{0,16},{4,20},{8,24},{12,28},{16,0},{20,4},{24,8},{28,12},{1,17},{... | collective-permute-start | bytes 2764808 | tf_op jit(solution)/shard_map/ppermute | solution.py:15
  24.9 14.4 %collective-permute-start.1 = (f32[5,1,32,1440]{3,2,1,0:T(8,128)S(1)}, f32[5,1,32,1440]{3,2,1,0:T(8,128)S(1)}, u32[]{:S(2)}, u32[]{:S(2)}) collective-permute-start(f32[5,1,32,1440]{3,2,1,0:T(8,128)S(1)} %collective-permute-done), channel_id=1, source_target_pairs={{0,4},{4,8},{8,12},{12,16},{16,20},{20,24},{24,28},{28,0},{1,5},{5... | collective-permute-start | bytes 2764808 | tf_op jit(solution)/shard_map/ppermute | solution.py:15
  39.6 23.1 %collective-permute-start.2 = (f32[5,1,32,1440]{3,2,1,0:T(8,128)S(1)}, f32[5,1,32,1440]{3,2,1,0:T(8,128)S(1)}, u32[]{:S(2)}, u32[]{:S(2)}) collective-permute-start(f32[5,1,32,1440]{3,2,1,0:T(8,128)S(1)} %broadcast_select_fusion), channel_id=1, source_target_pairs={{0,8},{4,12},{8,16},{12,20},{16,24},{20,28},{24,0},{28,4},{1,9},{5... | collective-permute-start | bytes 2764808 | tf_op jit(solution)/shard_map/ppermute | solution.py:15
  62.8 21.5 %copy-start.12 = (s32[128]{0:T(128)S(1)}, s32[128]{0:T(128)}, u32[]{:S(2)}) copy-start(s32[128]{0:T(128)} %param.9) | copy-start | bytes 1540
  62.8 21.6 %copy-start.10 = (f32[2,1,128]{2,1,0:T(1,128)S(1)}, f32[2,1,128]{2,1,0:T(1,128)}, u32[]{:S(2)}) copy-start(f32[2,1,128]{2,1,0:T(1,128)} %param.6) | copy-start | bytes 3076
  62.8 21.3 %collective-permute-start.3 = (f32[5,1,32,1440]{3,2,1,0:T(8,128)S(1)}, f32[5,1,32,1440]{3,2,1,0:T(8,128)S(1)}, u32[]{:S(2)}, u32[]{:S(2)}) collective-permute-start(f32[5,1,32,1440]{3,2,1,0:T(8,128)S(1)} %broadcast_select_fusion.1), channel_id=1, source_target_pairs={{0,16},{4,20},{8,24},{12,28},{16,0},{20,4},{24,8},{28,12},{1,17},{... | collective-permute-start | bytes 2764808 | tf_op jit(solution)/shard_map/ppermute | solution.py:15
  84.3 14.5 %collective-permute-start.4 = (f32[5,1,32,1440]{3,2,1,0:T(8,128)S(1)}, f32[5,1,32,1440]{3,2,1,0:T(8,128)S(1)}, u32[]{:S(2)}, u32[]{:S(2)}) collective-permute-start(f32[5,1,32,1440]{3,2,1,0:T(8,128)S(1)} %broadcast_select_fusion.2), channel_id=1, source_target_pairs={{0,4},{4,8},{8,12},{12,16},{16,20},{20,24},{24,28},{28,0},{1,5},{5... | collective-permute-start | bytes 2764808 | tf_op jit(solution)/shard_map/ppermute | solution.py:15
  107.5 20.3 %all-to-all-start = ((f32[8,20,1440]{2,1,0:T(8,128)}), f32[8,20,1440]{2,1,0:T(8,128)S(1)}, u32[]{:S(2)}, u32[]{:S(2)}) async-start(f32[8,20,1440]{2,1,0:T(8,128)} %all_to_all.52), calls=%async_computation | async-start | bytes 2359296 | tf_op jit(solution)/shard_map/all_to_all | solution.py:152
  134.0 2.8 copy-start.4
  142.4 1.2 copy-start.13
  154.8 2.9 copy-start.2
  154.8 2.9 copy-start.3
  161.7 3.7 copy-start.11
  161.7 20.4 %all-to-all-start.1 = ((f32[20,8,1440]{2,0,1:T(8,128)}), f32[20,8,1440]{2,0,1:T(8,128)S(1)}, u32[]{:S(2)}, u32[]{:S(2)}) async-start(f32[20,8,1440]{2,0,1:T(8,128)} %copy_select_fusion.1), calls=%async_computation.1 | async-start | bytes 2359296 | tf_op jit(solution)/shard_map/all_to_all | solution.py:155
  182.3 5.1 %collective-permute-start.5 = (f32[5,1,2,1440]{3,2,0,1:T(2,128)S(1)}, f32[5,1,2,1440]{3,2,0,1:T(2,128)S(1)}, u32[]{:S(2)}, u32[]{:S(2)}) collective-permute-start(f32[5,1,2,1440]{3,2,0,1:T(2,128)S(1)} %slice.334), channel_id=1, source_target_pairs={{0,1},{1,2},{2,3},{4,5},{5,6},{6,7},{8,9},{9,10},{10,11},{12,13},{... | collective-permute-start | bytes 172808 | tf_op jit(solution)/shard_map/ppermute | solution.py:21
  187.8 20.1 %copy-start.7 = (s32[32]{0:T(128)S(1)}, s32[32]{0:T(128)}, u32[]{:S(2)}) copy-start(s32[32]{0:T(128)} %get-tuple-element.57) | copy-start | bytes 388
  188.0 19.8 %collective-permute-start.6 = (f32[5,1,32,1440]{3,2,0,1:T(8,128)S(1)}, f32[5,1,32,1440]{3,2,0,1:T(8,128)S(1)}, u32[]{:S(2)}, u32[]{:S(2)}) collective-permute-start(f32[5,1,32,1440]{3,2,0,1:T(8,128)S(1)} %slice_subtract_fusion.1), channel_id=1, source_target_pairs={{0,16},{4,20},{8,24},{12,28},{16,0},{20,4},{24,8},{28,12},{1,17},{... | collective-permute-start | bytes 2764808 | tf_op jit(solution)/shard_map/ppermute | solution.py:15
  207.9 14.4 %collective-permute-start.7 = (f32[5,1,32,1440]{3,2,0,1:T(8,128)S(1)}, f32[5,1,32,1440]{3,2,0,1:T(8,128)S(1)}, u32[]{:S(2)}, u32[]{:S(2)}) collective-permute-start(f32[5,1,32,1440]{3,2,0,1:T(8,128)S(1)} %collective-permute-done.6), channel_id=1, source_target_pairs={{0,4},{4,8},{8,12},{12,16},{16,20},{20,24},{24,28},{28,0},{1,5},{5... | collective-permute-start | bytes 2764808 | tf_op jit(solution)/shard_map/ppermute | solution.py:15
  222.5 25.1 %collective-permute-start.8 = (f32[5,1,32,1440]{3,2,0,1:T(8,128)S(1)}, f32[5,1,32,1440]{3,2,0,1:T(8,128)S(1)}, u32[]{:S(2)}, u32[]{:S(2)}) collective-permute-start(f32[5,1,32,1440]{3,2,0,1:T(8,128)S(1)} %broadcast_select_fusion.3), channel_id=1, source_target_pairs={{0,8},{4,12},{8,16},{12,20},{16,24},{20,28},{24,0},{28,4},{1,9},{5... | collective-permute-start | bytes 2764808 | tf_op jit(solution)/shard_map/ppermute | solution.py:15
  247.8 23.5 %copy-start.8 = (s32[32]{0:T(128)S(1)}, s32[32]{0:T(128)}, u32[]{:S(2)}) copy-start(s32[32]{0:T(128)} %get-tuple-element.56) | copy-start | bytes 388
  247.8 23.3 %collective-permute-start.9 = (f32[5,1,32,1440]{3,2,0,1:T(8,128)S(1)}, f32[5,1,32,1440]{3,2,0,1:T(8,128)S(1)}, u32[]{:S(2)}, u32[]{:S(2)}) collective-permute-start(f32[5,1,32,1440]{3,2,0,1:T(8,128)S(1)} %broadcast_select_fusion.4), channel_id=1, source_target_pairs={{0,16},{4,20},{8,24},{12,28},{16,0},{20,4},{24,8},{28,12},{1,17},{... | collective-permute-start | bytes 2764808 | tf_op jit(solution)/shard_map/ppermute | solution.py:15
  271.3 14.5 %collective-permute-start.10 = (f32[5,1,32,1440]{3,2,0,1:T(8,128)S(1)}, f32[5,1,32,1440]{3,2,0,1:T(8,128)S(1)}, u32[]{:S(2)}, u32[]{:S(2)}) collective-permute-start(f32[5,1,32,1440]{3,2,0,1:T(8,128)S(1)} %broadcast_select_fusion.5), channel_id=1, source_target_pairs={{0,4},{4,8},{8,12},{12,16},{16,20},{20,24},{24,28},{28,0},{1,5},{5... | collective-permute-start | bytes 2764808 | tf_op jit(solution)/shard_map/ppermute | solution.py:15
  293.3 5.0 %copy-start.6 = (f32[32]{0:T(128)S(1)}, f32[32]{0:T(128)}, u32[]{:S(2)}) copy-start(f32[32]{0:T(128)} %get-tuple-element.61) | copy-start | bytes 388
  294.5 20.3 %all-to-all-start.2 = ((f32[8,20,1440]{2,1,0:T(8,128)}), f32[8,20,1440]{2,1,0:T(8,128)S(1)}, u32[]{:S(2)}, u32[]{:S(2)}) async-start(f32[8,20,1440]{2,1,0:T(8,128)} %all_to_all.59), calls=%async_computation.2 | async-start | bytes 2359296 | tf_op jit(solution)/shard_map/all_to_all | solution.py:152
  321.0 2.8 copy-start.5
  329.4 1.2 copy-start.14
  341.6 2.9 copy-start
  341.6 2.9 copy-start.1
  347.4 23.3 %copy-start.9 = (f32[1,128]{1,0:T(1,128)S(1)}, f32[1,128]{1,0:T(1,128)}, u32[]{:S(2)}) copy-start(f32[1,128]{1,0:T(1,128)} %get-tuple-element.23) | copy-start | bytes 1540
  366.8 5.8 %collective-permute-start.11 = (f32[5,1,2,1440]{3,2,0,1:T(2,128)S(1)}, f32[5,1,2,1440]{3,2,0,1:T(2,128)S(1)}, u32[]{:S(2)}, u32[]{:S(2)}) collective-permute-start(f32[5,1,2,1440]{3,2,0,1:T(2,128)S(1)} %slice.367), channel_id=1, source_target_pairs={{0,1},{1,2},{2,3},{4,5},{5,6},{6,7},{8,9},{9,10},{10,11},{12,13},{... | collective-permute-start | bytes 172808 | tf_op jit(solution)/shard_map/ppermute | solution.py:21
where the time goes:
time: 381 us; the launch traced here: 375 us
  waiting for transfers between devices  234 us (61%)
  matrix products  31.4 us (8%)
  local copies, waits for them, and re-layouts  30.5 us (8%)
  other arithmetic  29.7 us (8%)
  starting transfers between devices  27.9 us (7%)
  blocking collectives  19.2 us (5%)
    ppermute x10, waiting for transfers between devices, passed_along(): lax.ppermute(x, axis, [(i, (i + by) % devices) for i in range(devices)])  183 us
    all_to_all x2, waiting for transfers between devices, body(): whole = lax.all_to_all(flat, 'lon', split_axis=0, concat_axis=1, tiled=True)  31.3 us
    all_to_all x1, blocking collectives, body(): lax.all_to_all(whole, 'lon', split_axis=1, concat_axis=0, tiled=True)  19.2 us
    all_to_all x1, waiting for transfers between devices, body(): lax.all_to_all(whole, 'lon', split_axis=1, concat_axis=0, tiled=True)  16.2 us
    select_n x22, other arithmetic, roll_digits(): values = jnp.where(taken, moved, values)  11.1 us
    ppermute x10, starting transfers between devices, passed_along(): lax.ppermute(x, axis, [(i, (i + by) % devices) for i in range(devices)])  9.47 us
  transfers between devices with their start and end apart: 15, of which 15 were waited for; matrix products, arithmetic and copies ran while one was open for 1% of the time, Pallas kernels for 0%

commit v1 on v0

--- a/solution.py
+++ b/solution.py
@@ -152,7 +152,26 @@
         whole = lax.all_to_all(flat, "lon", split_axis=0, concat_axis=1, tiled=True)
         whole = zonal_fraction(whole, my_rows(fractions)[:, None])
         whole = polar_smooth(whole, row_lats, row_marks, lat_cells, lat_total)
-        blocks = lax.all_to_all(whole, "lon", split_axis=1, concat_axis=0, tiled=True)
+
+        def review_the_steps_all(local_block, axis_id="lon"):
+            spare = jax.lax.psum(1, axis_id)
+            w1 = jax.lax.axis_index(axis_id)
+            tall, small = (spare, w1)
+            s_next = local_block.shape[1] // tall
+            later = jnp.roll(local_block, -small * s_next, 1)
+            left_arr = lax.slice_in_dim(later, 0, s_next, axis=1)
+            i0 = 1
+            rack = [left_arr]
+            while i0 < tall:
+                o_now = lax.slice_in_dim(later, i0 * s_next, (i0 + 1) * s_next, axis=1)
+                rack.append(
+                    jax.lax.ppermute(o_now, axis_id, [(j, (j + i0) % tall) for j in range(tall)])
+                )
+                i0 = i0 + 1
+            mixed_arr = jnp.roll(jnp.concatenate(rack[::-1], 0), (small + 1) * rack[0].shape[0], 0)
+            return mixed_arr
+
+        blocks = review_the_steps_all(whole)
         state = blocks.reshape(n_fields, n_levels, lat_cells, lon_cells)
         state = meridional(state, frac_y[substep], first_row)
     return state

time: 381 us -> 366 us (0.961)
  blocking collectives: 19.2 us -> 0 us
  waiting for transfers between devices: 234 us -> 244 us
  local copies, waits for them, and re-layouts: 30.5 us -> 22.9 us
  starting transfers between devices: 27.9 us -> 35.3 us
    ppermute x0 -> x14, waiting for transfers between devices: none -> 21.6 us  [review_the_steps_all(): jax.lax.ppermute(o_now, axis_id, [(j, (j + i0) % tall) for j in range(tal...]
    all_to_all x1 -> x0, blocking collectives: 19.2 us -> none  [body(): lax.all_to_all(whole, 'lon', split_axis=1, concat_axis=0, tiled=True)]
    all_to_all x1 -> x0, waiting for transfers between devices: 16.2 us -> none  [body(): lax.all_to_all(whole, 'lon', split_axis=1, concat_axis=0, tiled=True)]
    ppermute x0 -> x14, starting transfers between devices: none -> 11 us  [review_the_steps_all(): jax.lax.ppermute(o_now, axis_id, [(j, (j + i0) % tall) for j in range(tal...]
    select_n x2, other arithmetic: 6.9 us -> 0.83 us  [polar_smooth(): return jnp.where((marks == 1)[:, None], result, whole)]
    div x2 -> x0, local copies, waits for them, and re-layouts: 5.86 us -> none  [polar_smooth(): result = result.reshape(row_count, lon_total) / lon_total]
  transfers between devices with their start and end apart: 15 -> 28, of which waited for: 15 -> 23; matrix products, arithmetic and copies ran while one was open for 1% -> 1% of each run, Pallas kernels for 0% -> 0%
where the time goes in v1:
time: 366 us; the launch traced here: 360 us
  waiting for transfers between devices  244 us (67%)
  starting transfers between devices  35.3 us (10%)
  matrix products  29.6 us (8%)
  other arithmetic  26.8 us (7%)
  local copies, waits for them, and re-layouts  22.9 us (6%)
    ppermute x10, waiting for transfers between devices, passed_along(): lax.ppermute(x, axis, [(i, (i + by) % devices) for i in range(devices)])  187 us
    all_to_all x2, waiting for transfers between devices, body(): whole = lax.all_to_all(flat, 'lon', split_axis=0, concat_axis=1, tiled=True)  31.9 us
    ppermute x14, waiting for transfers between devices, review_the_steps_all(): jax.lax.ppermute(o_now, axis_id, [(j, (j + i0) % tall) for j in range(tal...  21.6 us
    select_n x22, other arithmetic, roll_digits(): values = jnp.where(taken, moved, values)  11.1 us
    ppermute x14, starting transfers between devices, review_the_steps_all(): jax.lax.ppermute(o_now, axis_id, [(j, (j + i0) % tall) for j in range(tal...  11 us
    ppermute x10, starting transfers between devices, passed_along(): lax.ppermute(x, axis, [(i, (i + by) % devices) for i in range(devices)])  9.57 us
    all_to_all x2, starting transfers between devices, body(): whole = lax.all_to_all(flat, 'lon', split_axis=0, concat_axis=1, tiled=True)  7.55 us
    all_to_all x8, local copies, waits for them, and re-layouts, body(): whole = lax.all_to_all(flat, 'lon', split_axis=0, concat_axis=1, tiled=True)  7.42 us
  transfers between devices with their start and end apart: 28, of which 23 were waited for; matrix products, arithmetic and copies ran while one was open for 1% of the time, Pallas kernels for 0%

profile of v1, /device:TPU:0, one launch (start us, length us, event | category | flops | bytes accessed | tf_op | source)
XLA Modules:
  0.0 360.0 jit_solution(4594524290744521118)
XLA Ops:
  0.0 3.0 collective-permute-start
  3.0 22.0 %collective-permute-done = f32[5,1,32,1440]{3,2,1,0:T(8,128)S(1)} collective-permute-done((f32[5,1,32,1440]{3,2,1,0:T(8,128)}, f32[5,1,32,1440]{3,2,1,0:T(8,128)S(1)}, u32[]{:S(2)}, u32[]{:S(2)}) %collective-permute-start) | collective-permute-done | bytes 921632 | tf_op jit(solution)/shard_map/ppermute | solution.py:15
  25.7 13.6 %collective-permute-done.1 = f32[5,1,32,1440]{3,2,1,0:T(8,128)S(1)} collective-permute-done((f32[5,1,32,1440]{3,2,1,0:T(8,128)S(1)}, f32[5,1,32,1440]{3,2,1,0:T(8,128)S(1)}, u32[]{:S(2)}, u32[]{:S(2)}) %collective-permute-start.1) | collective-permute-done | bytes 921632 | tf_op jit(solution)/shard_map/ppermute | solution.py:15
  40.4 22.2 %collective-permute-done.2 = f32[5,1,32,1440]{3,2,1,0:T(8,128)S(1)} collective-permute-done((f32[5,1,32,1440]{3,2,1,0:T(8,128)S(1)}, f32[5,1,32,1440]{3,2,1,0:T(8,128)S(1)}, u32[]{:S(2)}, u32[]{:S(2)}) %collective-permute-start.2) | collective-permute-done | bytes 921632 | tf_op jit(solution)/shard_map/ppermute | solution.py:15
  62.8 1.6 collective-permute-start.3
  64.4 19.7 %collective-permute-done.3 = f32[5,1,32,1440]{3,2,1,0:T(8,128)S(1)} collective-permute-done((f32[5,1,32,1440]{3,2,1,0:T(8,128)S(1)}, f32[5,1,32,1440]{3,2,1,0:T(8,128)S(1)}, u32[]{:S(2)}, u32[]{:S(2)}) %collective-permute-start.3) | collective-permute-done | bytes 921632 | tf_op jit(solution)/shard_map/ppermute | solution.py:15
  84.7 14.1 %collective-permute-done.4 = f32[5,1,32,1440]{3,2,1,0:T(8,128)S(1)} collective-permute-done((f32[5,1,32,1440]{3,2,1,0:T(8,128)S(1)}, f32[5,1,32,1440]{3,2,1,0:T(8,128)S(1)}, u32[]{:S(2)}, u32[]{:S(2)}) %collective-permute-start.4) | collective-permute-done | bytes 921632 | tf_op jit(solution)/shard_map/ppermute | solution.py:15
  107.5 3.8 %all-to-all-start = ((f32[8,20,1440]{2,1,0:T(8,128)}), f32[8,20,1440]{2,1,0:T(8,128)S(1)}, u32[]{:S(2)}, u32[]{:S(2)}) async-start(f32[8,20,1440]{2,1,0:T(8,128)} %all_to_all.32), calls=%async_computation | async-start | bytes 2359296 | tf_op jit(solution)/shard_map/all_to_all | solution.py:152
  112.3 15.6 %all-to-all-done = f32[8,20,1440]{2,1,0:T(8,128)S(1)} async-done(((f32[8,20,1440]{2,1,0:T(8,128)}), f32[8,20,1440]{2,1,0:T(8,128)S(1)}, u32[]{:S(2)}, u32[]{:S(2)}) %all-to-all-start) | async-done | bytes 921632 | tf_op jit(solution)/shard_map/all_to_all | solution.py:152
  129.0 1.4 all_to_all.35
  130.9 1.3 pad_maximum_fusion.5
  132.2 2.4 concatenate.855
  135.8 2.3 multiply_subtract_fusion.3
  142.9 1.2 fusion.12
  145.2 1.6 fusion.11
  150.4 1.3 fusion.37
  151.7 1.3 fusion.10
  155.8 2.6 collective-permute-start.5
  158.4 1.5 collective-permute-start.6
  160.0 3.0 collective-permute-done.10
  163.4 4.8 %collective-permute-done.6 = f32[20,1440]{1,0:T(8,128)S(1)} collective-permute-done((f32[20,1440]{1,0:T(8,128)S(1)}, f32[20,1440]{1,0:T(8,128)S(1)}, u32[]{:S(2)}, u32[]{:S(2)}) %collective-permute-start.6) | collective-permute-done | bytes 115232 | tf_op jit(solution)/shard_map/ppermute | solution.py:168
  168.3 2.8 collective-permute-done.8
  172.2 3.3 collective-permute-start.12
  175.6 1.8 collective-permute-done.12
  178.5 21.8 %collective-permute-done.13 = f32[5,1,32,1440]{3,2,0,1:T(8,128)S(1)} collective-permute-done((f32[5,1,32,1440]{3,2,0,1:T(8,128)S(1)}, f32[5,1,32,1440]{3,2,0,1:T(8,128)S(1)}, u32[]{:S(2)}, u32[]{:S(2)}) %collective-permute-start.13) | collective-permute-done | bytes 921632 | tf_op jit(solution)/shard_map/ppermute | solution.py:15
  200.3 14.4 %collective-permute-done.14 = f32[5,1,32,1440]{3,2,0,1:T(8,128)S(1)} collective-permute-done((f32[5,1,32,1440]{3,2,0,1:T(8,128)S(1)}, f32[5,1,32,1440]{3,2,0,1:T(8,128)S(1)}, u32[]{:S(2)}, u32[]{:S(2)}) %collective-permute-start.14) | collective-permute-done | bytes 921632 | tf_op jit(solution)/shard_map/ppermute | solution.py:15
  214.9 2.8 collective-permute-start.15
  217.7 22.2 %collective-permute-done.15 = f32[5,1,32,1440]{3,2,0,1:T(8,128)S(1)} collective-permute-done((f32[5,1,32,1440]{3,2,0,1:T(8,128)S(1)}, f32[5,1,32,1440]{3,2,0,1:T(8,128)S(1)}, u32[]{:S(2)}, u32[]{:S(2)}) %collective-permute-start.15) | collective-permute-done | bytes 921632 | tf_op jit(solution)/shard_map/ppermute | solution.py:15
  240.6 22.8 %collective-permute-done.16 = f32[5,1,32,1440]{3,2,0,1:T(8,128)S(1)} collective-permute-done((f32[5,1,32,1440]{3,2,0,1:T(8,128)S(1)}, f32[5,1,32,1440]{3,2,0,1:T(8,128)S(1)}, u32[]{:S(2)}, u32[]{:S(2)}) %collective-permute-start.16) | collective-permute-done | bytes 921632 | tf_op jit(solution)/shard_map/ppermute | solution.py:15
  263.9 14.3 %collective-permute-done.17 = f32[5,1,32,1440]{3,2,0,1:T(8,128)S(1)} collective-permute-done((f32[5,1,32,1440]{3,2,0,1:T(8,128)S(1)}, f32[5,1,32,1440]{3,2,0,1:T(8,128)S(1)}, u32[]{:S(2)}, u32[]{:S(2)}) %collective-permute-start.17) | collective-permute-done | bytes 921632 | tf_op jit(solution)/shard_map/ppermute | solution.py:15
  286.9 3.8 %all-to-all-start.1 = ((f32[8,20,1440]{2,1,0:T(8,128)}), f32[8,20,1440]{2,1,0:T(8,128)S(1)}, u32[]{:S(2)}, u32[]{:S(2)}) async-start(f32[8,20,1440]{2,1,0:T(8,128)} %all_to_all.37), calls=%async_computation.1 | async-start | bytes 2359296 | tf_op jit(solution)/shard_map/all_to_all | solution.py:152
  290.9 16.4 %all-to-all-done.1 = f32[8,20,1440]{2,1,0:T(8,128)S(1)} async-done(((f32[8,20,1440]{2,1,0:T(8,128)}), f32[8,20,1440]{2,1,0:T(8,128)S(1)}, u32[]{:S(2)}, u32[]{:S(2)}) %all-to-all-start.1) | async-done | bytes 921632 | tf_op jit(solution)/shard_map/all_to_all | solution.py:152
  308.4 1.4 all_to_all.40
  310.3 1.3 pad_maximum_fusion.7
  311.7 2.4 concatenate.874
  315.2 2.3 multiply_subtract_fusion.1
  322.3 1.2 fusion.7
  324.6 1.2 fusion.6
  325.9 1.4 fusion.64
  329.6 1.3 fusion.30
  331.0 1.3 fusion.5
  338.7 1.9 collective-permute-start.23
  340.5 1.3 collective-permute-done.19
  342.2 1.4 collective-permute-done.20
  343.6 5.5 %collective-permute-done.21 = f32[20,1440]{1,0:T(8,128)S(1)} collective-permute-done((f32[20,1440]{1,0:T(8,128)S(1)}, f32[20,1440]{1,0:T(8,128)S(1)}, u32[]{:S(2)}, u32[]{:S(2)}) %collective-permute-start.21) | collective-permute-done | bytes 115232 | tf_op jit(solution)/shard_map/ppermute | solution.py:168
  349.1 2.0 collective-permute-done.22
  352.2 4.0 %collective-permute-start.25 = (f32[5,1,2,1440]{3,2,1,0:T(2,128)S(1)}, f32[5,1,2,1440]{3,2,1,0:T(2,128)S(1)}, u32[]{:S(2)}, u32[]{:S(2)}) collective-permute-start(f32[5,1,2,1440]{3,2,1,0:T(2,128)S(1)} %slice.447), channel_id=1, source_target_pairs={{0,1},{1,2},{2,3},{4,5},{5,6},{6,7},{8,9},{9,10},{10,11},{12,13},{... | collective-permute-start | bytes 172808 | tf_op jit(solution)/shard_map/ppermute | solution.py:21
  356.3 1.8 collective-permute-done.25
  (169 shorter events, 60.3 us)
Async XLA Ops:
  0.0 24.9 %collective-permute-start = (f32[5,1,32,1440]{3,2,1,0:T(8,128)}, f32[5,1,32,1440]{3,2,1,0:T(8,128)S(1)}, u32[]{:S(2)}, u32[]{:S(2)}) collective-permute-start(f32[5,1,32,1440]{3,2,1,0:T(8,128)} %param.9), channel_id=1, source_target_pairs={{0,16},{4,20},{8,24},{12,28},{16,0},{20,4},{24,8},{28,12},{1,17},{... | collective-permute-start | bytes 2764808 | tf_op jit(solution)/shard_map/ppermute | solution.py:15
  24.9 14.4 %collective-permute-start.1 = (f32[5,1,32,1440]{3,2,1,0:T(8,128)S(1)}, f32[5,1,32,1440]{3,2,1,0:T(8,128)S(1)}, u32[]{:S(2)}, u32[]{:S(2)}) collective-permute-start(f32[5,1,32,1440]{3,2,1,0:T(8,128)S(1)} %collective-permute-done), channel_id=1, source_target_pairs={{0,4},{4,8},{8,12},{12,16},{16,20},{20,24},{24,28},{28,0},{1,5},{5... | collective-permute-start | bytes 2764808 | tf_op jit(solution)/shard_map/ppermute | solution.py:15
  39.6 23.1 %collective-permute-start.2 = (f32[5,1,32,1440]{3,2,1,0:T(8,128)S(1)}, f32[5,1,32,1440]{3,2,1,0:T(8,128)S(1)}, u32[]{:S(2)}, u32[]{:S(2)}) collective-permute-start(f32[5,1,32,1440]{3,2,1,0:T(8,128)S(1)} %broadcast_select_fusion), channel_id=1, source_target_pairs={{0,8},{4,12},{8,16},{12,20},{16,24},{20,28},{24,0},{28,4},{1,9},{5... | collective-permute-start | bytes 2764808 | tf_op jit(solution)/shard_map/ppermute | solution.py:15
  62.8 21.5 %copy-start.2 = (s32[128]{0:T(128)S(1)}, s32[128]{0:T(128)}, u32[]{:S(2)}) copy-start(s32[128]{0:T(128)} %param.13) | copy-start | bytes 1540
  62.8 21.6 %copy-start = (f32[2,1,128]{2,1,0:T(1,128)S(1)}, f32[2,1,128]{2,1,0:T(1,128)}, u32[]{:S(2)}) copy-start(f32[2,1,128]{2,1,0:T(1,128)} %param.10) | copy-start | bytes 3076
  62.8 21.3 %collective-permute-start.3 = (f32[5,1,32,1440]{3,2,1,0:T(8,128)S(1)}, f32[5,1,32,1440]{3,2,1,0:T(8,128)S(1)}, u32[]{:S(2)}, u32[]{:S(2)}) collective-permute-start(f32[5,1,32,1440]{3,2,1,0:T(8,128)S(1)} %broadcast_select_fusion.1), channel_id=1, source_target_pairs={{0,16},{4,20},{8,24},{12,28},{16,0},{20,4},{24,8},{28,12},{1,17},{... | collective-permute-start | bytes 2764808 | tf_op jit(solution)/shard_map/ppermute | solution.py:15
  84.3 14.5 %collective-permute-start.4 = (f32[5,1,32,1440]{3,2,1,0:T(8,128)S(1)}, f32[5,1,32,1440]{3,2,1,0:T(8,128)S(1)}, u32[]{:S(2)}, u32[]{:S(2)}) collective-permute-start(f32[5,1,32,1440]{3,2,1,0:T(8,128)S(1)} %broadcast_select_fusion.2), channel_id=1, source_target_pairs={{0,4},{4,8},{8,12},{12,16},{16,20},{20,24},{24,28},{28,0},{1,5},{5... | collective-permute-start | bytes 2764808 | tf_op jit(solution)/shard_map/ppermute | solution.py:15
  107.5 20.3 %all-to-all-start = ((f32[8,20,1440]{2,1,0:T(8,128)}), f32[8,20,1440]{2,1,0:T(8,128)S(1)}, u32[]{:S(2)}, u32[]{:S(2)}) async-start(f32[8,20,1440]{2,1,0:T(8,128)} %all_to_all.32), calls=%async_computation | async-start | bytes 2359296 | tf_op jit(solution)/shard_map/all_to_all | solution.py:152
  154.3 9.1 %copy-start.1 = (f32[2,1,128]{2,1,0:T(1,128)S(1)}, f32[2,1,128]{2,1,0:T(1,128)}, u32[]{:S(2)}) copy-start(f32[2,1,128]{2,1,0:T(1,128)} %param.11) | copy-start | bytes 3076
  155.2 7.7 %collective-permute-start.10 = (f32[20,1440]{1,0:T(8,128)S(1)}, f32[20,1440]{1,0:T(8,128)S(1)}, u32[]{:S(2)}, u32[]{:S(2)}) collective-permute-start(f32[20,1440]{1,0:T(8,128)S(1)} %get-tuple-element.35), channel_id=1, source_target_pairs={{0,8},{4,12},{8,16},{12,20},{16,24},{20,28},{24,0},{28,4},{1,9},{5... | collective-permute-start | bytes 345608 | tf_op jit(solution)/shard_map/ppermute | solution.py:168
  155.8 7.6 %collective-permute-start.11 = (f32[20,1440]{1,0:T(8,128)S(1)}, f32[20,1440]{1,0:T(8,128)S(1)}, u32[]{:S(2)}, u32[]{:S(2)}) collective-permute-start(f32[20,1440]{1,0:T(8,128)S(1)} %get-tuple-element.34), channel_id=1, source_target_pairs={{0,4},{4,8},{8,12},{12,16},{16,20},{20,24},{24,28},{28,0},{1,5},{5... | collective-permute-start | bytes 345608 | tf_op jit(solution)/shard_map/ppermute | solution.py:168
  155.8 7.6 %collective-permute-start.5 = (f32[20,1440]{1,0:T(8,128)S(1)}, f32[20,1440]{1,0:T(8,128)S(1)}, u32[]{:S(2)}, u32[]{:S(2)}) collective-permute-start(f32[20,1440]{1,0:T(8,128)S(1)} %get-tuple-element.40), channel_id=1, source_target_pairs={{0,28},{4,0},{8,4},{12,8},{16,12},{20,16},{24,20},{28,24},{1,29},{... | collective-permute-start | bytes 345608 | tf_op jit(solution)/shard_map/ppermute | solution.py:168
  158.4 9.8 %collective-permute-start.6 = (f32[20,1440]{1,0:T(8,128)S(1)}, f32[20,1440]{1,0:T(8,128)S(1)}, u32[]{:S(2)}, u32[]{:S(2)}) collective-permute-start(f32[20,1440]{1,0:T(8,128)S(1)} %get-tuple-element.39), channel_id=1, source_target_pairs={{0,24},{4,28},{8,0},{12,4},{16,8},{20,12},{24,16},{28,20},{1,25},{... | collective-permute-start | bytes 345608 | tf_op jit(solution)/shard_map/ppermute | solution.py:168
  160.0 8.4 %collective-permute-start.7 = (f32[20,1440]{1,0:T(8,128)S(1)}, f32[20,1440]{1,0:T(8,128)S(1)}, u32[]{:S(2)}, u32[]{:S(2)}) collective-permute-start(f32[20,1440]{1,0:T(8,128)S(1)} %get-tuple-element.38), channel_id=1, source_target_pairs={{0,20},{4,24},{8,28},{12,0},{16,4},{20,8},{24,12},{28,16},{1,21},{... | collective-permute-start | bytes 345608 | tf_op jit(solution)/shard_map/ppermute | solution.py:168
  162.9 8.2 %collective-permute-start.8 = (f32[20,1440]{1,0:T(8,128)S(1)}, f32[20,1440]{1,0:T(8,128)S(1)}, u32[]{:S(2)}, u32[]{:S(2)}) collective-permute-start(f32[20,1440]{1,0:T(8,128)S(1)} %get-tuple-element.37), channel_id=1, source_target_pairs={{0,16},{4,20},{8,24},{12,28},{16,0},{20,4},{24,8},{28,12},{1,17},{... | collective-permute-start | bytes 345608 | tf_op jit(solution)/shard_map/ppermute | solution.py:168
  163.4 7.7 %collective-permute-start.9 = (f32[20,1440]{1,0:T(8,128)S(1)}, f32[20,1440]{1,0:T(8,128)S(1)}, u32[]{:S(2)}, u32[]{:S(2)}) collective-permute-start(f32[20,1440]{1,0:T(8,128)S(1)} %get-tuple-element.36), channel_id=1, source_target_pairs={{0,12},{4,16},{8,20},{12,24},{16,28},{20,0},{24,4},{28,8},{1,13},{... | collective-permute-start | bytes 345608 | tf_op jit(solution)/shard_map/ppermute | solution.py:168
  172.2 5.1 %collective-permute-start.12 = (f32[5,1,2,1440]{3,2,0,1:T(2,128)S(1)}, f32[5,1,2,1440]{3,2,0,1:T(2,128)S(1)}, u32[]{:S(2)}, u32[]{:S(2)}) collective-permute-start(f32[5,1,2,1440]{3,2,0,1:T(2,128)S(1)} %slice.406), channel_id=1, source_target_pairs={{0,1},{1,2},{2,3},{4,5},{5,6},{6,7},{8,9},{9,10},{10,11},{12,13},{... | collective-permute-start | bytes 172808 | tf_op jit(solution)/shard_map/ppermute | solution.py:21
  177.9 22.4 %collective-permute-start.13 = (f32[5,1,32,1440]{3,2,0,1:T(8,128)S(1)}, f32[5,1,32,1440]{3,2,0,1:T(8,128)S(1)}, u32[]{:S(2)}, u32[]{:S(2)}) collective-permute-start(f32[5,1,32,1440]{3,2,0,1:T(8,128)S(1)} %slice_subtract_fusion.1), channel_id=1, source_target_pairs={{0,16},{4,20},{8,24},{12,28},{16,0},{20,4},{24,8},{28,12},{1,17},{... | collective-permute-start | bytes 2764808 | tf_op jit(solution)/shard_map/ppermute | solution.py:15
  200.3 14.4 %collective-permute-start.14 = (f32[5,1,32,1440]{3,2,0,1:T(8,128)S(1)}, f32[5,1,32,1440]{3,2,0,1:T(8,128)S(1)}, u32[]{:S(2)}, u32[]{:S(2)}) collective-permute-start(f32[5,1,32,1440]{3,2,0,1:T(8,128)S(1)} %collective-permute-done.13), channel_id=1, source_target_pairs={{0,4},{4,8},{8,12},{12,16},{16,20},{20,24},{24,28},{28,0},{1,5},{5... | collective-permute-start | bytes 2764808 | tf_op jit(solution)/shard_map/ppermute | solution.py:15
  214.9 25.0 %collective-permute-start.15 = (f32[5,1,32,1440]{3,2,0,1:T(8,128)S(1)}, f32[5,1,32,1440]{3,2,0,1:T(8,128)S(1)}, u32[]{:S(2)}, u32[]{:S(2)}) collective-permute-start(f32[5,1,32,1440]{3,2,0,1:T(8,128)S(1)} %broadcast_select_fusion.3), channel_id=1, source_target_pairs={{0,8},{4,12},{8,16},{12,20},{16,24},{20,28},{24,0},{28,4},{1,9},{5... | collective-permute-start | bytes 2764808 | tf_op jit(solution)/shard_map/ppermute | solution.py:15
  240.1 23.3 %collective-permute-start.16 = (f32[5,1,32,1440]{3,2,0,1:T(8,128)S(1)}, f32[5,1,32,1440]{3,2,0,1:T(8,128)S(1)}, u32[]{:S(2)}, u32[]{:S(2)}) collective-permute-start(f32[5,1,32,1440]{3,2,0,1:T(8,128)S(1)} %broadcast_select_fusion.4), channel_id=1, source_target_pairs={{0,16},{4,20},{8,24},{12,28},{16,0},{20,4},{24,8},{28,12},{1,17},{... | collective-permute-start | bytes 2764808 | tf_op jit(solution)/shard_map/ppermute | solution.py:15
  263.6 14.6 %collective-permute-start.17 = (f32[5,1,32,1440]{3,2,0,1:T(8,128)S(1)}, f32[5,1,32,1440]{3,2,0,1:T(8,128)S(1)}, u32[]{:S(2)}, u32[]{:S(2)}) collective-permute-start(f32[5,1,32,1440]{3,2,0,1:T(8,128)S(1)} %broadcast_select_fusion.5), channel_id=1, source_target_pairs={{0,4},{4,8},{8,12},{12,16},{16,20},{20,24},{24,28},{28,0},{1,5},{5... | collective-permute-start | bytes 2764808 | tf_op jit(solution)/shard_map/ppermute | solution.py:15
  286.9 20.3 %all-to-all-start.1 = ((f32[8,20,1440]{2,1,0:T(8,128)}), f32[8,20,1440]{2,1,0:T(8,128)S(1)}, u32[]{:S(2)}, u32[]{:S(2)}) async-start(f32[8,20,1440]{2,1,0:T(8,128)} %all_to_all.37), calls=%async_computation.1 | async-start | bytes 2359296 | tf_op jit(solution)/shard_map/all_to_all | solution.py:152
  334.4 4.2 %collective-permute-start.18 = (f32[20,1440]{1,0:T(8,128)S(1)}, f32[20,1440]{1,0:T(8,128)S(1)}, u32[]{:S(2)}, u32[]{:S(2)}) collective-permute-start(f32[20,1440]{1,0:T(8,128)S(1)} %get-tuple-element.32), channel_id=1, source_target_pairs={{0,28},{4,0},{8,4},{12,8},{16,12},{20,16},{24,20},{28,24},{1,29},{... | collective-permute-start | bytes 345608 | tf_op jit(solution)/shard_map/ppermute | solution.py:168
  334.5 7.3 %collective-permute-start.19 = (f32[20,1440]{1,0:T(8,128)S(1)}, f32[20,1440]{1,0:T(8,128)S(1)}, u32[]{:S(2)}, u32[]{:S(2)}) collective-permute-start(f32[20,1440]{1,0:T(8,128)S(1)} %get-tuple-element.31), channel_id=1, source_target_pairs={{0,24},{4,28},{8,0},{12,4},{16,8},{20,12},{24,16},{28,20},{1,25},{... | collective-permute-start | bytes 345608 | tf_op jit(solution)/shard_map/ppermute | solution.py:168
  335.2 8.4 %collective-permute-start.20 = (f32[20,1440]{1,0:T(8,128)S(1)}, f32[20,1440]{1,0:T(8,128)S(1)}, u32[]{:S(2)}, u32[]{:S(2)}) collective-permute-start(f32[20,1440]{1,0:T(8,128)S(1)} %get-tuple-element.30), channel_id=1, source_target_pairs={{0,20},{4,24},{8,28},{12,0},{16,4},{20,8},{24,12},{28,16},{1,21},{... | collective-permute-start | bytes 345608 | tf_op jit(solution)/shard_map/ppermute | solution.py:168
  336.3 12.8 %collective-permute-start.21 = (f32[20,1440]{1,0:T(8,128)S(1)}, f32[20,1440]{1,0:T(8,128)S(1)}, u32[]{:S(2)}, u32[]{:S(2)}) collective-permute-start(f32[20,1440]{1,0:T(8,128)S(1)} %get-tuple-element.29), channel_id=1, source_target_pairs={{0,16},{4,20},{8,24},{12,28},{16,0},{20,4},{24,8},{28,12},{1,17},{... | collective-permute-start | bytes 345608 | tf_op jit(solution)/shard_map/ppermute | solution.py:168
  337.0 14.2 %collective-permute-start.22 = (f32[20,1440]{1,0:T(8,128)S(1)}, f32[20,1440]{1,0:T(8,128)S(1)}, u32[]{:S(2)}, u32[]{:S(2)}) collective-permute-start(f32[20,1440]{1,0:T(8,128)S(1)} %get-tuple-element.28), channel_id=1, source_target_pairs={{0,12},{4,16},{8,20},{12,24},{16,28},{20,0},{24,4},{28,8},{1,13},{... | collective-permute-start | bytes 345608 | tf_op jit(solution)/shard_map/ppermute | solution.py:168
  338.7 12.5 %collective-permute-start.23 = (f32[20,1440]{1,0:T(8,128)S(1)}, f32[20,1440]{1,0:T(8,128)S(1)}, u32[]{:S(2)}, u32[]{:S(2)}) collective-permute-start(f32[20,1440]{1,0:T(8,128)S(1)} %get-tuple-element.27), channel_id=1, source_target_pairs={{0,8},{4,12},{8,16},{12,20},{16,24},{20,28},{24,0},{28,4},{1,9},{5... | collective-permute-start | bytes 345608 | tf_op jit(solution)/shard_map/ppermute | solution.py:168
  341.8 9.3 %collective-permute-start.24 = (f32[20,1440]{1,0:T(8,128)S(1)}, f32[20,1440]{1,0:T(8,128)S(1)}, u32[]{:S(2)}, u32[]{:S(2)}) collective-permute-start(f32[20,1440]{1,0:T(8,128)S(1)} %get-tuple-element.26), channel_id=1, source_target_pairs={{0,4},{4,8},{8,12},{12,16},{16,20},{20,24},{24,28},{28,0},{1,5},{5... | collective-permute-start | bytes 345608 | tf_op jit(solution)/shard_map/ppermute | solution.py:168
  352.2 5.8 %collective-permute-start.25 = (f32[5,1,2,1440]{3,2,1,0:T(2,128)S(1)}, f32[5,1,2,1440]{3,2,1,0:T(2,128)S(1)}, u32[]{:S(2)}, u32[]{:S(2)}) collective-permute-start(f32[5,1,2,1440]{3,2,1,0:T(2,128)S(1)} %slice.447), channel_id=1, source_target_pairs={{0,1},{1,2},{2,3},{4,5},{5,6},{6,7},{8,9},{9,10},{10,11},{12,13},{... | collective-permute-start | bytes 172808 | tf_op jit(solution)/shard_map/ppermute | solution.py:21
